TPU v7x, 512 devices: a whole 4x8x8 slice. The times are simulated.
512 devices in a mesh: row: 32 (over z, y_hi, core), col: 16 (over y_lo, x).
Axes of the slice: x: 4, y: 8 (y_hi: 2, y_lo: 4; y = y_hi * 4 + y_lo), z: 8, core: 2. Of those that a mesh axis runs over, the one named last changes fastest.
Arguments:
- patches: bfloat16 [1024, 1024, 256], P('row', 'col'), may hold values from -6 to 6
- norm_gain: float32 [256], replicated, may hold values from 0.1 to 1.9
- w_first: bfloat16 [2, 4, 64, 64], replicated, may hold values from -0.5 to 0.5
- w_second: bfloat16 [2, 4, 64, 64], replicated, may hold values from -0.5 to 0.5
- depth_kernel: float32 [3, 3, 256], replicated, may hold values from -2 to 2
Outputs:
- mixed: bfloat16 [1024, 1024, 256], P('row', 'col')
All inputs are finite; a program needn't handle non-finite values.
Results may differ from a plain program's by a relative error of at most 0.008.
Values may be sent and summed in bfloat16 or wider, within the bound.
No kernel may reach another device: no remote copies, remote signals or barrier semaphores. Data moves between devices by JAX's collectives and lax.ppermute only.
A program may use at most 64 MiB of HBM per device.

v0:
```python
import math
import jax
import jax.numpy as jnp
from jax import lax
from jax.sharding import PartitionSpec as P


def with_halo(shard, sides, width):
    for axis, dim in sides:
        devices, length = (lax.axis_size(axis), shard.shape[dim])
        up = [(i, (i + 1) % devices) for i in range(devices)]
        down = [(j, i) for i, j in up]
        last = lax.slice_in_dim(shard, length - width, length, axis=dim)
        leading = lax.slice_in_dim(shard, 0, width, axis=dim)
        before = lax.ppermute(last, axis, up)
        after = lax.ppermute(leading, axis, down)
        shard = jnp.concatenate([before, shard, after], axis=dim)
    return shard


def phase_table(first_idx, second_idx, length):
    product = first_idx[:, None] * second_idx[None, :] % length
    phase = product.astype(jnp.float32) * (2.0 * math.pi / length)
    return (jnp.cos(phase).astype(jnp.bfloat16), jnp.sin(phase).astype(jnp.bfloat16))


def shrink(values):
    level = 0.25
    return jnp.where(
        values > level, values - level, jnp.where(values < -level, values + level, 0.0 * values)
    )


def block_product(left, weight):
    return jnp.einsum("qmbc,bcd->qmbd", left, weight, preferred_element_type=jnp.float32)


def local(patches, norm_gain, w_first, w_second, depth_kernel):
    n_row = lax.axis_size("row")
    n_col = lax.axis_size("col")
    rows_dev, cols_dev, chans = patches.shape
    patch_grid_height = rows_dev * n_row
    grid_w = cols_dev * n_col
    half = grid_w // 2
    blocks = w_first.shape[1]
    width = w_first.shape[2]
    width_factors = 1.0 / math.sqrt(grid_w)
    height_factors = 1.0 / math.sqrt(patch_grid_height)
    xf = patches.astype(jnp.float32)
    mean = jnp.mean(xf, axis=-1, keepdims=True)
    var = jnp.mean((xf - mean) ** 2, axis=-1, keepdims=True)
    normed = ((xf - mean) * lax.rsqrt(var + 1e-05) * norm_gain).astype(jnp.bfloat16)
    padded = with_halo(normed, (("row", 0), ("col", 1)), 1)
    conv = jnp.zeros((rows_dev, cols_dev, chans), jnp.float32)
    for i in range(3):
        for j in range(3):
            conv = conv + padded[i : i + rows_dev, j : j + cols_dev] * depth_kernel[i, j]
    strips = lax.all_to_all(normed, "col", split_axis=0, concat_axis=1, tiled=True)
    cos_w, sin_w = phase_table(
        jnp.arange(grid_w, dtype=jnp.int32), jnp.arange(half, dtype=jnp.int32), grid_w
    )
    forward_w = jnp.concatenate([cos_w, -sin_w], axis=1)
    spectrum_values = jnp.einsum(
        "hwc,wk->hkc", strips, forward_w, preferred_element_type=jnp.float32
    )
    spectrum_values = (spectrum_values * width_factors).astype(jnp.bfloat16)
    wre = spectrum_values[:, :half]
    wim = spectrum_values[:, half:]
    positions = jnp.arange(patch_grid_height, dtype=jnp.int32)
    across_re, across_im = (
        lax.all_to_all(wre, "col", split_axis=1, concat_axis=0, tiled=True),
        lax.all_to_all(wim, "col", split_axis=1, concat_axis=0, tiled=True),
    )
    full_re, full_im = (
        lax.all_to_all(across_re, "row", split_axis=1, concat_axis=0, tiled=True),
        lax.all_to_all(across_im, "row", split_axis=1, concat_axis=0, tiled=True),
    )
    cos_h, sin_h = phase_table(positions, positions, patch_grid_height)
    big_table = jnp.concatenate(
        [jnp.concatenate([cos_h, sin_h], axis=1), jnp.concatenate([-sin_h, cos_h], axis=1)], axis=0
    )
    stacked = jnp.concatenate([full_re, full_im], axis=0)
    spectrum = jnp.einsum("qp,pmc->qmc", big_table, stacked, preferred_element_type=jnp.float32)
    spectrum = (spectrum * height_factors).astype(jnp.bfloat16)
    modes = spectrum.shape[1]
    zre = spectrum[:patch_grid_height].reshape(patch_grid_height, modes, blocks, width)
    zim = spectrum[patch_grid_height:].reshape(patch_grid_height, modes, blocks, width)
    hre = jnp.tanh(block_product(zre, w_first[0]) - block_product(zim, w_first[1])).astype(
        jnp.bfloat16
    )
    him = jnp.tanh(block_product(zre, w_first[1]) + block_product(zim, w_first[0])).astype(
        jnp.bfloat16
    )
    spectrum_real = shrink(
        block_product(hre, w_second[0]) - block_product(him, w_second[1])
    ).astype(jnp.bfloat16)
    spectrum_imaginary = shrink(
        block_product(hre, w_second[1]) + block_product(him, w_second[0])
    ).astype(jnp.bfloat16)
    filtered = jnp.concatenate(
        [
            spectrum_real.reshape(patch_grid_height, modes, chans),
            spectrum_imaginary.reshape(patch_grid_height, modes, chans),
        ],
        axis=0,
    )
    inverse_transform = jnp.einsum(
        "qp,qmc->pmc", big_table, filtered, preferred_element_type=jnp.float32
    )
    inverse_transform = (inverse_transform * height_factors).astype(jnp.bfloat16)
    value_real = inverse_transform[:patch_grid_height]
    value_imaginary = inverse_transform[patch_grid_height:]
    part_re, part_im = (
        lax.all_to_all(value_real, "row", split_axis=0, concat_axis=1, tiled=True),
        lax.all_to_all(value_imaginary, "row", split_axis=0, concat_axis=1, tiled=True),
    )
    line_re, line_im = (
        lax.all_to_all(part_re, "col", split_axis=0, concat_axis=1, tiled=True),
        lax.all_to_all(part_im, "col", split_axis=0, concat_axis=1, tiled=True),
    )
    filter_coefficient = jnp.where(jnp.arange(half) == 0, 1.0, 2.0).astype(jnp.float32)
    inverse_w = jnp.concatenate(
        [
            (cos_w.astype(jnp.float32) * filter_coefficient).T,
            -(sin_w.astype(jnp.float32) * filter_coefficient).T,
        ],
        axis=0,
    ).astype(jnp.bfloat16)
    lines = jnp.concatenate([line_re, line_im], axis=1)
    spectral = jnp.einsum("hkc,kw->hwc", lines, inverse_w, preferred_element_type=jnp.float32)
    spectral = (spectral * width_factors).astype(jnp.bfloat16)
    home = lax.all_to_all(spectral, "col", split_axis=1, concat_axis=0, tiled=True)
    return (xf + home.astype(jnp.float32) + conv).astype(jnp.bfloat16)


def solution(mesh):
    return jax.shard_map(
        local,
        mesh=mesh,
        in_specs=(P("row", "col", None), P(), P(), P(), P()),
        out_specs=P("row", "col", None),
        check_vma=False,
    )
```

profile of v0, /device:TPU:63, one launch (start us, length us, event | category | flops | bytes accessed | tf_op | source)
XLA Modules:
  0.0 328.7 jit_solution(4939369207946088311)
XLA Ops:
  0.0 1.7 convert_reduce_fusion
  1.7 1.9 fusion.10
  3.6 1.5 fusion.12
  5.1 6.9 %all-to-all-start = ((bf16[32,64,256]{2,1,0:T(8,128)(2,1)}), bf16[32,64,256]{2,1,0:T(8,128)(2,1)S(1)}, u32[]{:S(2)}, u32[]{:S(2)}) async-start(bf16[32,64,256]{2,1,0:T(8,128)(2,1)} %fusion.12), calls=%async_computation | async-start | bytes 2097152 | tf_op jit(solution)/shard_map/all_to_all | solution.py:58
  12.1 7.8 %cosine_convert_fusion.1 = bf16[1024,512]{0,1:T(8,128)(2,1)S(1)} fusion(), kind=kLoop, calls=%fused_computation.50 | loop fusion | flops 7864320 | bytes 1048576 | tf_op jit(solution)/shard_map/convert_element_type | solution.py:24
  19.8 8.6 %fusion.41 = bf16[1024,512]{0,1:T(8,128)(2,1)} fusion(), kind=kLoop, calls=%fused_computation.75 | loop fusion | flops 9437184 | bytes 1048576 | tf_op jit(solution)/shard_map/neg | solution.py:62
  28.4 6.1 %all-to-all-done = bf16[32,64,256]{2,1,0:T(8,128)(2,1)S(1)} async-done(((bf16[32,64,256]{2,1,0:T(8,128)(2,1)}), bf16[32,64,256]{2,1,0:T(8,128)(2,1)S(1)}, u32[]{:S(2)}, u32[]{:S(2)}) %all-to-all-start) | async-done | bytes 1048608 | tf_op jit(solution)/shard_map/all_to_all | solution.py:58
  34.6 1.1 copy-done.3
  35.7 1.3 fusion.33
  37.1 1.3 copy.51
  38.4 7.4 %all-to-all-start.1 = ((bf16[2,512,256]{2,0,1:T(2,128)(2,1)}), bf16[2,512,256]{2,0,1:T(2,128)(2,1)S(1)}, u32[]{:S(2)}, u32[]{:S(2)}) async-start(bf16[2,512,256]{2,0,1:T(2,128)(2,1)} %copy.51), calls=%async_computation.1 | async-start | bytes 1048576 | tf_op jit(solution)/shard_map/all_to_all | solution.py:71
  45.8 1.3 copy.55
  47.1 10.5 %all-to-all-done.1 = bf16[2,512,256]{2,0,1:T(2,128)(2,1)S(1)} async-done(((bf16[2,512,256]{2,0,1:T(2,128)(2,1)}), bf16[2,512,256]{2,0,1:T(2,128)(2,1)S(1)}, u32[]{:S(2)}, u32[]{:S(2)}) %all-to-all-start.1) | async-done | bytes 524320 | tf_op jit(solution)/shard_map/all_to_all | solution.py:71
  57.7 6.7 %all-to-all-start.3 = ((bf16[2,512,256]{2,0,1:T(2,128)(2,1)}), bf16[2,512,256]{2,0,1:T(2,128)(2,1)S(1)}, u32[]{:S(2)}, u32[]{:S(2)}) async-start(bf16[2,512,256]{2,0,1:T(2,128)(2,1)} %copy.55), calls=%async_computation.3 | async-start | bytes 1048576 | tf_op jit(solution)/shard_map/all_to_all | solution.py:72
  64.5 1.1 copy.54
  65.5 10.0 %all-to-all-done.3 = bf16[2,512,256]{2,0,1:T(2,128)(2,1)S(1)} async-done(((bf16[2,512,256]{2,0,1:T(2,128)(2,1)}), bf16[2,512,256]{2,0,1:T(2,128)(2,1)S(1)}, u32[]{:S(2)}, u32[]{:S(2)}) %all-to-all-start.3) | async-done | bytes 524320 | tf_op jit(solution)/shard_map/all_to_all | solution.py:72
  75.5 17.7 %all-to-all-start.2 = ((bf16[32,32,256]{2,0,1:T(8,128)(2,1)}), bf16[32,32,256]{2,0,1:T(8,128)(2,1)S(1)}, u32[]{:S(2)}, u32[]{:S(2)}) async-start(bf16[32,32,256]{2,0,1:T(8,128)(2,1)} %copy.54), calls=%async_computation.2 | async-start | bytes 1048576 | tf_op jit(solution)/shard_map/all_to_all | solution.py:75
  93.3 1.1 copy.58
  94.4 16.0 %all-to-all-done.2 = bf16[32,32,256]{2,0,1:T(8,128)(2,1)S(1)} async-done(((bf16[32,32,256]{2,0,1:T(8,128)(2,1)}), bf16[32,32,256]{2,0,1:T(8,128)(2,1)S(1)}, u32[]{:S(2)}, u32[]{:S(2)}) %all-to-all-start.2) | async-done | bytes 524320 | tf_op jit(solution)/shard_map/all_to_all | solution.py:75
  110.4 0.8 copy-done.5
  111.2 8.0 %all-to-all-start.4 = ((bf16[32,32,256]{2,0,1:T(8,128)(2,1)}), bf16[32,32,256]{2,0,1:T(8,128)(2,1)}, u32[]{:S(2)}, u32[]{:S(2)}) async-start(bf16[32,32,256]{2,0,1:T(8,128)(2,1)} %copy.58), calls=%async_computation.4 | async-start | bytes 1048576 | tf_op jit(solution)/shard_map/all_to_all | solution.py:76
  119.2 15.8 %fusion.49 = bf16[1024,1024]{1,0:T(8,128)(2,1)S(1)} fusion(), kind=kLoop, calls=%fused_computation.89 | loop fusion | flops 18874368 | bytes 2097152 | tf_op jit(solution)/shard_map/neg | solution.py:80
  135.1 17.7 %sine_convert_fusion = (bf16[1024,1024]{1,0:T(8,128)(2,1)}, bf16[1024,1024]{1,0:T(8,128)(2,1)}) fusion(), kind=kLoop, calls=%fused_computation.7 | loop fusion | flops 16777216 | bytes 4194304 | tf_op jit(solution)/shard_map/convert_element_type | solution.py:24
  152.8 14.9 %fusion.6 = bf16[2048,256]{0,1:T(8,128)(2,1)S(1)} fusion(bf16[1024,1024]{1,0:T(8,128)(2,1)} %get-tuple-element.29, bf16[1024,1024]{1,0:T(8,128)(2,1)S(1)} %fusion.49, bf16[1024,1024]{1,0:T(8,128)(2,1)} %get-tuple-element.28, bf16[1024,1,256]{2,0,1:T(8,128)(2,1)} %bitcast.17, bf16[1024,1,256]{2,0,1:T(8,128)(2,1)} %bitcast.166), kind=kOutput, calls=%fused_computation.23 | convolution fusion | flops 2184183808 | bytes 8388608 | tf_op jit(solution)/shard_map/qp,pmc->qmc/dot_general | solution.py:83
  167.7 0.8 copy-done.4
  170.9 0.5 select_convert_fusion.1
  171.9 0.6 copy-done.1
  172.4 0.6 copy-done.2
  173.1 2.4 fusion.7
  175.5 0.5 broadcast.174
  176.1 1.0 reduce.1
  177.3 0.9 reshape.124
  178.2 12.2 %all-to-all-start.5 = ((bf16[32,2,4096]{2,1,0:T(2,128)(2,1)}), bf16[32,2,4096]{2,1,0:T(2,128)(2,1)S(1)}, u32[]{:S(2)}, u32[]{:S(2)}) async-start(bf16[32,2,4096]{2,1,0:T(2,128)(2,1)} %reshape.124), calls=%async_computation.5 | async-start | bytes 1048576 | tf_op jit(solution)/shard_map/all_to_all | solution.py:114
  190.4 1.0 reduce
  191.7 0.9 reshape.122
  192.6 14.9 %all-to-all-done.5 = bf16[32,2,4096]{2,1,0:T(2,128)(2,1)S(1)} async-done(((bf16[32,2,4096]{2,1,0:T(2,128)(2,1)}), bf16[32,2,4096]{2,1,0:T(2,128)(2,1)S(1)}, u32[]{:S(2)}, u32[]{:S(2)}) %all-to-all-start.5) | async-done | bytes 524320 | tf_op jit(solution)/shard_map/all_to_all | solution.py:114
  207.5 8.0 %all-to-all-start.7 = ((bf16[32,2,4096]{2,1,0:T(2,128)(2,1)}), bf16[32,2,4096]{2,1,0:T(2,128)(2,1)S(1)}, u32[]{:S(2)}, u32[]{:S(2)}) async-start(bf16[32,2,4096]{2,1,0:T(2,128)(2,1)} %reshape.122), calls=%async_computation.7 | async-start | bytes 1048576 | tf_op jit(solution)/shard_map/all_to_all | solution.py:115
  215.5 0.5 reshape.125
  216.1 1.1 copy.65
  217.3 15.3 %all-to-all-done.7 = bf16[32,2,4096]{2,1,0:T(2,128)(2,1)S(1)} async-done(((bf16[32,2,4096]{2,1,0:T(2,128)(2,1)}), bf16[32,2,4096]{2,1,0:T(2,128)(2,1)S(1)}, u32[]{:S(2)}, u32[]{:S(2)}) %all-to-all-start.7) | async-done | bytes 524320 | tf_op jit(solution)/shard_map/all_to_all | solution.py:115
  232.6 7.9 %all-to-all-start.6 = ((bf16[32,32,256]{2,1,0:T(8,128)(2,1)}), bf16[32,32,256]{2,1,0:T(8,128)(2,1)S(1)}, u32[]{:S(2)}, u32[]{:S(2)}) async-start(bf16[32,32,256]{2,1,0:T(8,128)(2,1)} %copy.65), calls=%async_computation.6 | async-start | bytes 1048576 | tf_op jit(solution)/shard_map/all_to_all | solution.py:118
  240.5 0.5 reshape.123
  241.2 1.1 copy.68
  242.2 10.2 %all-to-all-done.6 = bf16[32,32,256]{2,1,0:T(8,128)(2,1)S(1)} async-done(((bf16[32,32,256]{2,1,0:T(8,128)(2,1)}), bf16[32,32,256]{2,1,0:T(8,128)(2,1)S(1)}, u32[]{:S(2)}, u32[]{:S(2)}) %all-to-all-start.6) | async-done | bytes 524320 | tf_op jit(solution)/shard_map/all_to_all | solution.py:118
  252.4 6.9 %all-to-all-start.8 = ((bf16[32,32,256]{2,1,0:T(8,128)(2,1)}), bf16[32,32,256]{2,1,0:T(8,128)(2,1)S(1)}, u32[]{:S(2)}, u32[]{:S(2)}) async-start(bf16[32,32,256]{2,1,0:T(8,128)(2,1)} %copy.68), calls=%async_computation.8 | async-start | bytes 1048576 | tf_op jit(solution)/shard_map/all_to_all | solution.py:119
  259.3 9.4 %multiply_convert_fusion.2 = (bf16[512,1024]{0,1:T(8,128)(2,1)S(1)}, bf16[512,1024]{0,1:T(8,128)(2,1)}) fusion(f32[512]{0:T(512)S(1)} %fusion.70), kind=kLoop, calls=%fused_computation.55 | loop fusion | flops 12058624 | bytes 2099200 | tf_op jit(solution)/shard_map/convert.7
  268.7 0.9 copy.66
  269.6 1.4 all-to-all-done.8
  271.1 2.6 fusion.34
  273.7 2.0 copy.70
  275.7 6.8 %all-to-all-start.9 = ((bf16[2,1024,256]{2,0,1:T(2,128)(2,1)}), bf16[2,1024,256]{2,0,1:T(2,128)(2,1)}, u32[]{:S(2)}, u32[]{:S(2)}) async-start(bf16[2,1024,256]{2,0,1:T(2,128)(2,1)} %copy.70), calls=%async_computation.9 | async-start | bytes 2097152 | tf_op jit(solution)/shard_map/all_to_all | solution.py:132
  282.5 0.8 fusion.75
  283.3 8.8 %collective-permute-start = (bf16[1,64,256]{2,1,0:T(8,128)(2,1)S(1)}, bf16[1,64,256]{2,1,0:T(8,128)(2,1)S(1)}, u32[]{:S(2)}, u32[]{:S(2)}) collective-permute-start(bf16[1,64,256]{2,1,0:T(8,128)(2,1)S(1)} %get-tuple-element.9), channel_id=1, source_target_pairs={{0,16},{16,32},{32,48},{48,64},{64,80},{80,96},{96,112},{112,128},... | collective-permute-start | bytes 98312 | tf_op jit(solution)/shard_map/ppermute | solution.py:15
  292.2 1.9 collective-permute-start.1
  294.1 4.3 %collective-permute-done = bf16[1,64,256]{2,1,0:T(8,128)(2,1)S(1)} collective-permute-done((bf16[1,64,256]{2,1,0:T(8,128)(2,1)S(1)}, bf16[1,64,256]{2,1,0:T(8,128)(2,1)S(1)}, u32[]{:S(2)}, u32[]{:S(2)}) %collective-permute-start) | collective-permute-done | bytes 32800 | tf_op jit(solution)/shard_map/ppermute | solution.py:15
  298.4 8.2 %collective-permute-done.1 = bf16[1,64,256]{2,1,0:T(8,128)(2,1)S(1)} collective-permute-done((bf16[1,64,256]{2,1,0:T(8,128)(2,1)S(1)}, bf16[1,64,256]{2,1,0:T(8,128)(2,1)S(1)}, u32[]{:S(2)}, u32[]{:S(2)}) %collective-permute-start.1) | collective-permute-done | bytes 32800 | tf_op jit(solution)/shard_map/ppermute | solution.py:16
  306.6 1.0 pad_maximum_fusion.5
  307.6 1.9 collective-permute-start.2
  309.6 3.6 %collective-permute-start.3 = (bf16[34,1,256]{2,1,0:T(2,128)(2,1)S(1)}, bf16[34,1,256]{2,1,0:T(2,128)(2,1)S(1)}, u32[]{:S(2)}, u32[]{:S(2)}) collective-permute-start(bf16[34,1,256]{2,1,0:T(2,128)(2,1)S(1)} %get-tuple-element.8), channel_id=1, source_target_pairs={{1,0},{2,1},{3,2},{4,3},{5,4},{6,5},{7,6},{8,7},{9,8},{10,9},{11,1... | collective-permute-start | bytes 52232 | tf_op jit(solution)/shard_map/ppermute | solution.py:16
  313.2 0.6 fusion.78
  313.8 4.3 %collective-permute-done.3 = bf16[34,1,256]{2,1,0:T(2,128)(2,1)S(1)} collective-permute-done((bf16[34,1,256]{2,1,0:T(2,128)(2,1)S(1)}, bf16[34,1,256]{2,1,0:T(2,128)(2,1)S(1)}, u32[]{:S(2)}, u32[]{:S(2)}) %collective-permute-start.3) | collective-permute-done | bytes 17440 | tf_op jit(solution)/shard_map/ppermute | solution.py:16
  318.2 2.3 maximum_maximum_fusion.3
  320.5 2.1 convert_bitcast_fusion
  323.4 5.2 %fusion.14 = bf16[32,64,256]{2,1,0:T(8,128)(2,1)} fusion(bf16[32,64,256]{2,1,0:T(8,128)(2,1)S(1)} %copy-done, f32[16,2,64,256]{3,2,1,0:T(8,128)S(1)} %copy.71, bf16[32,64,256]{2,1,0:T(8,128)(2,1)} %fusion.12, bf16[34,65,256]{2,1,0:T(8,128)(2,1)S(1)} %get-tuple-element.6, bf16[1,64,256]{2,1,0:T(8,128)(2,1)S(1)} %copy-done.9, ...), kind=kLoop, calls=%fused_computation.31 | loop fusion | flops 16777216 | bytes 11609088 | tf_op jit(solution)/shard_map/convert_element_type | solution.py:133
  (66 shorter events, 4.6 us)
Async XLA Ops:
  0.0 3.6 %copy-start = (bf16[32,64,256]{2,1,0:T(8,128)(2,1)S(1)}, bf16[32,64,256]{2,1,0:T(8,128)(2,1)}, u32[]{:S(2)}) copy-start(bf16[32,64,256]{2,1,0:T(8,128)(2,1)} %param.5) | copy-start | bytes 3145732
  0.0 3.6 %copy-start.21 = (f32[256]{0:T(256)S(1)}, f32[256]{0:T(256)}, u32[]{:S(2)}) copy-start(f32[256]{0:T(256)} %param.6) | copy-start | bytes 3076
  5.1 29.4 %all-to-all-start = ((bf16[32,64,256]{2,1,0:T(8,128)(2,1)}), bf16[32,64,256]{2,1,0:T(8,128)(2,1)S(1)}, u32[]{:S(2)}, u32[]{:S(2)}) async-start(bf16[32,64,256]{2,1,0:T(8,128)(2,1)} %fusion.12), calls=%async_computation | async-start | bytes 2097152 | tf_op jit(solution)/shard_map/all_to_all | solution.py:58
  34.5 1.2 copy-start.3
  38.4 19.3 %all-to-all-start.1 = ((bf16[2,512,256]{2,0,1:T(2,128)(2,1)}), bf16[2,512,256]{2,0,1:T(2,128)(2,1)S(1)}, u32[]{:S(2)}, u32[]{:S(2)}) async-start(bf16[2,512,256]{2,0,1:T(2,128)(2,1)} %copy.51), calls=%async_computation.1 | async-start | bytes 1048576 | tf_op jit(solution)/shard_map/all_to_all | solution.py:71
  57.7 17.8 %all-to-all-start.3 = ((bf16[2,512,256]{2,0,1:T(2,128)(2,1)}), bf16[2,512,256]{2,0,1:T(2,128)(2,1)S(1)}, u32[]{:S(2)}, u32[]{:S(2)}) async-start(bf16[2,512,256]{2,0,1:T(2,128)(2,1)} %copy.55), calls=%async_computation.3 | async-start | bytes 1048576 | tf_op jit(solution)/shard_map/all_to_all | solution.py:72
  75.5 34.8 %all-to-all-start.2 = ((bf16[32,32,256]{2,0,1:T(8,128)(2,1)}), bf16[32,32,256]{2,0,1:T(8,128)(2,1)S(1)}, u32[]{:S(2)}, u32[]{:S(2)}) async-start(bf16[32,32,256]{2,0,1:T(8,128)(2,1)} %copy.54), calls=%async_computation.2 | async-start | bytes 1048576 | tf_op jit(solution)/shard_map/all_to_all | solution.py:75
  110.3 0.8 copy-start.5
  111.2 41.6 %all-to-all-start.4 = ((bf16[32,32,256]{2,0,1:T(8,128)(2,1)}), bf16[32,32,256]{2,0,1:T(8,128)(2,1)}, u32[]{:S(2)}, u32[]{:S(2)}) async-start(bf16[32,32,256]{2,0,1:T(8,128)(2,1)} %copy.58), calls=%async_computation.4 | async-start | bytes 1048576 | tf_op jit(solution)/shard_map/all_to_all | solution.py:76
  167.6 0.9 copy-start.4
  168.9 0.9 copy-start.10
  170.8 1.6 copy-start.1
  170.9 2.2 copy-start.2
  178.2 29.3 %all-to-all-start.5 = ((bf16[32,2,4096]{2,1,0:T(2,128)(2,1)}), bf16[32,2,4096]{2,1,0:T(2,128)(2,1)S(1)}, u32[]{:S(2)}, u32[]{:S(2)}) async-start(bf16[32,2,4096]{2,1,0:T(2,128)(2,1)} %reshape.124), calls=%async_computation.5 | async-start | bytes 1048576 | tf_op jit(solution)/shard_map/all_to_all | solution.py:114
  207.5 25.1 %all-to-all-start.7 = ((bf16[32,2,4096]{2,1,0:T(2,128)(2,1)}), bf16[32,2,4096]{2,1,0:T(2,128)(2,1)S(1)}, u32[]{:S(2)}, u32[]{:S(2)}) async-start(bf16[32,2,4096]{2,1,0:T(2,128)(2,1)} %reshape.122), calls=%async_computation.7 | async-start | bytes 1048576 | tf_op jit(solution)/shard_map/all_to_all | solution.py:115
  232.6 19.8 %all-to-all-start.6 = ((bf16[32,32,256]{2,1,0:T(8,128)(2,1)}), bf16[32,32,256]{2,1,0:T(8,128)(2,1)S(1)}, u32[]{:S(2)}, u32[]{:S(2)}) async-start(bf16[32,32,256]{2,1,0:T(8,128)(2,1)} %copy.65), calls=%async_computation.6 | async-start | bytes 1048576 | tf_op jit(solution)/shard_map/all_to_all | solution.py:118
  252.4 18.6 %all-to-all-start.8 = ((bf16[32,32,256]{2,1,0:T(8,128)(2,1)}), bf16[32,32,256]{2,1,0:T(8,128)(2,1)S(1)}, u32[]{:S(2)}, u32[]{:S(2)}) async-start(bf16[32,32,256]{2,1,0:T(8,128)(2,1)} %copy.68), calls=%async_computation.8 | async-start | bytes 1048576 | tf_op jit(solution)/shard_map/all_to_all | solution.py:119
  275.7 37.5 %copy-start.11 = (f32[3,3,256]{2,1,0:T(4,128)S(1)}, f32[3,3,256]{2,1,0:T(4,128)}, u32[]{:S(2)}) copy-start(f32[3,3,256]{2,1,0:T(4,128)} %param.9) | copy-start | bytes 27652
  275.7 44.7 %all-to-all-start.9 = ((bf16[2,1024,256]{2,0,1:T(2,128)(2,1)}), bf16[2,1024,256]{2,0,1:T(2,128)(2,1)}, u32[]{:S(2)}, u32[]{:S(2)}) async-start(bf16[2,1024,256]{2,0,1:T(2,128)(2,1)} %copy.70), calls=%async_computation.9 | async-start | bytes 2097152 | tf_op jit(solution)/shard_map/all_to_all | solution.py:132
  283.3 15.0 %collective-permute-start = (bf16[1,64,256]{2,1,0:T(8,128)(2,1)S(1)}, bf16[1,64,256]{2,1,0:T(8,128)(2,1)S(1)}, u32[]{:S(2)}, u32[]{:S(2)}) collective-permute-start(bf16[1,64,256]{2,1,0:T(8,128)(2,1)S(1)} %get-tuple-element.9), channel_id=1, source_target_pairs={{0,16},{16,32},{32,48},{48,64},{64,80},{80,96},{96,112},{112,128},... | collective-permute-start | bytes 98312 | tf_op jit(solution)/shard_map/ppermute | solution.py:15
  292.2 14.4 %collective-permute-start.1 = (bf16[1,64,256]{2,1,0:T(8,128)(2,1)S(1)}, bf16[1,64,256]{2,1,0:T(8,128)(2,1)S(1)}, u32[]{:S(2)}, u32[]{:S(2)}) collective-permute-start(bf16[1,64,256]{2,1,0:T(8,128)(2,1)S(1)} %get-tuple-element.10), channel_id=1, source_target_pairs={{16,0},{32,16},{48,32},{64,48},{80,64},{96,80},{112,96},{128,112},... | collective-permute-start | bytes 98312 | tf_op jit(solution)/shard_map/ppermute | solution.py:16
  298.4 19.8 %copy-start.6 = (bf16[1,64,256]{2,1,0:T(8,128)(2,1)}, bf16[1,64,256]{2,1,0:T(8,128)(2,1)S(1)}, u32[]{:S(2)}) copy-start(bf16[1,64,256]{2,1,0:T(8,128)(2,1)S(1)} %collective-permute-done) | copy-start | bytes 98308
  306.6 11.6 %copy-start.8 = (bf16[1,64,256]{2,1,0:T(8,128)(2,1)}, bf16[1,64,256]{2,1,0:T(8,128)(2,1)S(1)}, u32[]{:S(2)}) copy-start(bf16[1,64,256]{2,1,0:T(8,128)(2,1)S(1)} %collective-permute-done.1) | copy-start | bytes 98308
  307.6 6.2 %collective-permute-start.2 = (bf16[34,1,256]{2,1,0:T(2,128)(2,1)S(1)}, bf16[34,1,256]{2,1,0:T(2,128)(2,1)S(1)}, u32[]{:S(2)}, u32[]{:S(2)}) collective-permute-start(bf16[34,1,256]{2,1,0:T(2,128)(2,1)S(1)} %get-tuple-element.7), channel_id=1, source_target_pairs={{0,1},{1,2},{2,3},{3,4},{4,5},{5,6},{6,7},{7,8},{8,9},{9,10},{10,1... | collective-permute-start | bytes 52232 | tf_op jit(solution)/shard_map/ppermute | solution.py:15
  309.6 8.6 %collective-permute-start.3 = (bf16[34,1,256]{2,1,0:T(2,128)(2,1)S(1)}, bf16[34,1,256]{2,1,0:T(2,128)(2,1)S(1)}, u32[]{:S(2)}, u32[]{:S(2)}) collective-permute-start(bf16[34,1,256]{2,1,0:T(2,128)(2,1)S(1)} %get-tuple-element.8), channel_id=1, source_target_pairs={{1,0},{2,1},{3,2},{4,3},{5,4},{6,5},{7,6},{8,7},{9,8},{10,9},{11,1... | collective-permute-start | bytes 52232 | tf_op jit(solution)/shard_map/ppermute | solution.py:16
  322.6 0.8 copy-start.7
  322.6 0.8 copy-start.9
  322.6 0.8 copy-start.12
  322.6 0.8 copy-start.13
  322.6 0.7 copy-start.14
  322.7 0.7 copy-start.15
  322.7 0.7 copy-start.16
  322.7 0.7 copy-start.17
  322.7 0.7 copy-start.18
  322.7 0.7 copy-start.19
  322.7 0.7 copy-start.20
where the time goes:
time: 330 us; the launch traced here: 329 us
  starting transfers between devices  105 us (32%)
  waiting for transfers between devices  101 us (31%)
  other arithmetic  77.1 us (23%)
  matrix products  24.2 us (7%)
  local copies, waits for them, and re-layouts  20.7 us (6%)
    convert_element_type x1, other arithmetic, phase_table(): jnp.sin(phase).astype(jnp.bfloat16)  17.7 us
    all_to_all x1, starting transfers between devices, local(): lax.all_to_all(across_re, 'row', split_axis=1, concat_axis=0, tiled=True)  17.7 us
    all_to_all x1, waiting for transfers between devices, local(): lax.all_to_all(across_re, 'row', split_axis=1, concat_axis=0, tiled=True)  16 us
    neg x1, other arithmetic, local(): -sin_h  15.8 us
    all_to_all x1, waiting for transfers between devices, local(): lax.all_to_all(value_imaginary, 'row', split_axis=0, concat_axis=1, tiled...  15.3 us
    all_to_all x1, waiting for transfers between devices, local(): lax.all_to_all(value_real, 'row', split_axis=0, concat_axis=1, tiled=True)  14.9 us
    dot_general x1, matrix products, local(): jnp.einsum('qp,pmc->qmc', big_table, stacked, preferred_element_type=jnp....  14.9 us
    ppermute x2, waiting for transfers between devices, with_halo(): after = lax.ppermute(leading, axis, down)  12.5 us
  transfers between devices with their start and end apart: 14, of which 11 were waited for; matrix products, arithmetic and copies ran while one was open for 23% of the time, Pallas kernels for 0%

commit v1 on v0

--- a/solution.py
+++ b/solution.py
@@ -114,8 +114,14 @@
         lax.all_to_all(value_real, "row", split_axis=0, concat_axis=1, tiled=True),
         lax.all_to_all(value_imaginary, "row", split_axis=0, concat_axis=1, tiled=True),
     )
+    pair_cards = lambda peer_axis, chunk: jnp.concatenate(
+        lax.all_to_all(
+            jnp.stack(jnp.split(chunk, lax.axis_size(peer_axis), axis=0), axis=0), peer_axis, 0, 0
+        ),
+        axis=1,
+    )
     line_re, line_im = (
-        lax.all_to_all(part_re, "col", split_axis=0, concat_axis=1, tiled=True),
+        pair_cards("col", chunk=part_re),
         lax.all_to_all(part_im, "col", split_axis=0, concat_axis=1, tiled=True),
     )
     filter_coefficient = jnp.where(jnp.arange(half) == 0, 1.0, 2.0).astype(jnp.float32)

time: 330 us -> 330 us (level)
  local copies, waits for them, and re-layouts: 20.7 us -> 29.8 us
  waiting for transfers between devices: 101 us -> 92.2 us
    unnamed x52 -> x67, local copies, waits for them, and re-layouts: 8.08 us -> 17.6 us
    all_to_all x1, waiting for transfers between devices: 15.3 us -> 6.29 us  [local(): lax.all_to_all(value_imaginary, 'row', split_axis=0, concat_axis=1, tiled...]
  transfers between devices with their start and end apart: 14 -> 14, of which waited for: 11 -> 11; matrix products, arithmetic and copies ran while one was open for 23% -> 25% of each run, Pallas kernels for 0% -> 0%
where the time goes in v1:
time: 330 us; the launch traced here: 329 us
  starting transfers between devices  105 us (32%)
  waiting for transfers between devices  92.2 us (28%)
  other arithmetic  77.1 us (23%)
  local copies, waits for them, and re-layouts  29.8 us (9%)
  matrix products  24.2 us (7%)
    convert_element_type x1, other arithmetic, phase_table(): jnp.sin(phase).astype(jnp.bfloat16)  17.7 us
    all_to_all x1, starting transfers between devices, local(): lax.all_to_all(across_re, 'row', split_axis=1, concat_axis=0, tiled=True)  17.7 us
    unnamed x67, local copies, waits for them, and re-layouts  17.6 us
    all_to_all x1, waiting for transfers between devices, local(): lax.all_to_all(across_re, 'row', split_axis=1, concat_axis=0, tiled=True)  16 us
    neg x1, other arithmetic, local(): -sin_h  15.8 us
    all_to_all x1, waiting for transfers between devices, local(): lax.all_to_all(value_real, 'row', split_axis=0, concat_axis=1, tiled=True)  14.9 us
    dot_general x1, matrix products, local(): jnp.einsum('qp,pmc->qmc', big_table, stacked, preferred_element_type=jnp....  14.9 us
    ppermute x2, waiting for transfers between devices, with_halo(): after = lax.ppermute(leading, axis, down)  12.8 us
  transfers between devices with their start and end apart: 14, of which 11 were waited for; matrix products, arithmetic and copies ran while one was open for 25% of the time, Pallas kernels for 0%

profile of v1, /device:TPU:63, one launch (start us, length us, event | category | flops | bytes accessed | tf_op | source)
XLA Modules:
  0.0 328.7 jit_solution(14973742373270852814)
XLA Ops:
  0.0 1.7 convert_reduce_fusion
  1.7 1.9 fusion.10
  3.6 1.5 fusion.12
  5.1 6.9 %all-to-all-start = ((bf16[32,64,256]{2,1,0:T(8,128)(2,1)}), bf16[32,64,256]{2,1,0:T(8,128)(2,1)S(1)}, u32[]{:S(2)}, u32[]{:S(2)}) async-start(bf16[32,64,256]{2,1,0:T(8,128)(2,1)} %fusion.12), calls=%async_computation | async-start | bytes 2097152 | tf_op jit(solution)/shard_map/all_to_all | solution.py:58
  12.1 7.8 %cosine_convert_fusion.1 = bf16[1024,512]{0,1:T(8,128)(2,1)S(1)} fusion(), kind=kLoop, calls=%fused_computation.50 | loop fusion | flops 7864320 | bytes 1048576 | tf_op jit(solution)/shard_map/convert_element_type | solution.py:24
  19.8 8.6 %fusion.41 = bf16[1024,512]{0,1:T(8,128)(2,1)} fusion(), kind=kLoop, calls=%fused_computation.75 | loop fusion | flops 9437184 | bytes 1048576 | tf_op jit(solution)/shard_map/neg | solution.py:62
  28.4 6.1 %all-to-all-done = bf16[32,64,256]{2,1,0:T(8,128)(2,1)S(1)} async-done(((bf16[32,64,256]{2,1,0:T(8,128)(2,1)}), bf16[32,64,256]{2,1,0:T(8,128)(2,1)S(1)}, u32[]{:S(2)}, u32[]{:S(2)}) %all-to-all-start) | async-done | bytes 1048608 | tf_op jit(solution)/shard_map/all_to_all | solution.py:58
  34.6 1.1 copy-done.3
  35.7 1.3 fusion.33
  37.1 1.3 copy.49
  38.4 7.4 %all-to-all-start.1 = ((bf16[2,512,256]{2,0,1:T(2,128)(2,1)}), bf16[2,512,256]{2,0,1:T(2,128)(2,1)S(1)}, u32[]{:S(2)}, u32[]{:S(2)}) async-start(bf16[2,512,256]{2,0,1:T(2,128)(2,1)} %copy.49), calls=%async_computation.1 | async-start | bytes 1048576 | tf_op jit(solution)/shard_map/all_to_all | solution.py:71
  45.8 1.3 copy.53
  47.1 10.5 %all-to-all-done.1 = bf16[2,512,256]{2,0,1:T(2,128)(2,1)S(1)} async-done(((bf16[2,512,256]{2,0,1:T(2,128)(2,1)}), bf16[2,512,256]{2,0,1:T(2,128)(2,1)S(1)}, u32[]{:S(2)}, u32[]{:S(2)}) %all-to-all-start.1) | async-done | bytes 524320 | tf_op jit(solution)/shard_map/all_to_all | solution.py:71
  57.7 6.7 %all-to-all-start.3 = ((bf16[2,512,256]{2,0,1:T(2,128)(2,1)}), bf16[2,512,256]{2,0,1:T(2,128)(2,1)S(1)}, u32[]{:S(2)}, u32[]{:S(2)}) async-start(bf16[2,512,256]{2,0,1:T(2,128)(2,1)} %copy.53), calls=%async_computation.3 | async-start | bytes 1048576 | tf_op jit(solution)/shard_map/all_to_all | solution.py:72
  64.5 1.1 copy.52
  65.5 10.0 %all-to-all-done.3 = bf16[2,512,256]{2,0,1:T(2,128)(2,1)S(1)} async-done(((bf16[2,512,256]{2,0,1:T(2,128)(2,1)}), bf16[2,512,256]{2,0,1:T(2,128)(2,1)S(1)}, u32[]{:S(2)}, u32[]{:S(2)}) %all-to-all-start.3) | async-done | bytes 524320 | tf_op jit(solution)/shard_map/all_to_all | solution.py:72
  75.5 17.7 %all-to-all-start.2 = ((bf16[32,32,256]{2,0,1:T(8,128)(2,1)}), bf16[32,32,256]{2,0,1:T(8,128)(2,1)S(1)}, u32[]{:S(2)}, u32[]{:S(2)}) async-start(bf16[32,32,256]{2,0,1:T(8,128)(2,1)} %copy.52), calls=%async_computation.2 | async-start | bytes 1048576 | tf_op jit(solution)/shard_map/all_to_all | solution.py:75
  93.3 1.1 copy.56
  94.4 16.0 %all-to-all-done.2 = bf16[32,32,256]{2,0,1:T(8,128)(2,1)S(1)} async-done(((bf16[32,32,256]{2,0,1:T(8,128)(2,1)}), bf16[32,32,256]{2,0,1:T(8,128)(2,1)S(1)}, u32[]{:S(2)}, u32[]{:S(2)}) %all-to-all-start.2) | async-done | bytes 524320 | tf_op jit(solution)/shard_map/all_to_all | solution.py:75
  110.4 0.8 copy-done.5
  111.2 8.0 %all-to-all-start.4 = ((bf16[32,32,256]{2,0,1:T(8,128)(2,1)}), bf16[32,32,256]{2,0,1:T(8,128)(2,1)}, u32[]{:S(2)}, u32[]{:S(2)}) async-start(bf16[32,32,256]{2,0,1:T(8,128)(2,1)} %copy.56), calls=%async_computation.4 | async-start | bytes 1048576 | tf_op jit(solution)/shard_map/all_to_all | solution.py:76
  119.2 15.8 %fusion.49 = bf16[1024,1024]{1,0:T(8,128)(2,1)S(1)} fusion(), kind=kLoop, calls=%fused_computation.89 | loop fusion | flops 18874368 | bytes 2097152 | tf_op jit(solution)/shard_map/neg | solution.py:80
  135.1 17.7 %sine_convert_fusion = (bf16[1024,1024]{1,0:T(8,128)(2,1)}, bf16[1024,1024]{1,0:T(8,128)(2,1)}) fusion(), kind=kLoop, calls=%fused_computation.7 | loop fusion | flops 16777216 | bytes 4194304 | tf_op jit(solution)/shard_map/convert_element_type | solution.py:24
  152.8 14.9 %fusion.6 = bf16[2048,256]{0,1:T(8,128)(2,1)S(1)} fusion(bf16[1024,1024]{1,0:T(8,128)(2,1)} %get-tuple-element.29, bf16[1024,1024]{1,0:T(8,128)(2,1)S(1)} %fusion.49, bf16[1024,1024]{1,0:T(8,128)(2,1)} %get-tuple-element.28, bf16[1024,1,256]{2,0,1:T(8,128)(2,1)} %bitcast.17, bf16[1024,1,256]{2,0,1:T(8,128)(2,1)} %bitcast.241), kind=kOutput, calls=%fused_computation.23 | convolution fusion | flops 2184183808 | bytes 8388608 | tf_op jit(solution)/shard_map/qp,pmc->qmc/dot_general | solution.py:83
  167.7 0.8 copy-done.4
  173.1 2.4 fusion.7
  176.1 1.0 reduce.1
  177.3 0.9 reshape.164
  178.2 12.2 %all-to-all-start.5 = ((bf16[32,2,4096]{2,1,0:T(2,128)(2,1)}), bf16[32,2,4096]{2,1,0:T(2,128)(2,1)S(1)}, u32[]{:S(2)}, u32[]{:S(2)}) async-start(bf16[32,2,4096]{2,1,0:T(2,128)(2,1)} %reshape.164), calls=%async_computation.5 | async-start | bytes 1048576 | tf_op jit(solution)/shard_map/all_to_all | solution.py:114
  190.4 1.0 reduce
  191.7 0.9 reshape.162
  192.6 14.9 %all-to-all-done.5 = bf16[32,2,4096]{2,1,0:T(2,128)(2,1)S(1)} async-done(((bf16[32,2,4096]{2,1,0:T(2,128)(2,1)}), bf16[32,2,4096]{2,1,0:T(2,128)(2,1)S(1)}, u32[]{:S(2)}, u32[]{:S(2)}) %all-to-all-start.5) | async-done | bytes 524320 | tf_op jit(solution)/shard_map/all_to_all | solution.py:114
  207.5 8.0 %all-to-all-start.7 = ((bf16[32,2,4096]{2,1,0:T(2,128)(2,1)}), bf16[32,2,4096]{2,1,0:T(2,128)(2,1)S(1)}, u32[]{:S(2)}, u32[]{:S(2)}) async-start(bf16[32,2,4096]{2,1,0:T(2,128)(2,1)} %reshape.162), calls=%async_computation.7 | async-start | bytes 1048576 | tf_op jit(solution)/shard_map/all_to_all | solution.py:115
  216.8 0.6 constant_dynamic-update-slice_fusion.14
  218.0 0.6 constant_dynamic-update-slice_fusion.12
  219.3 0.6 constant_dynamic-update-slice_fusion.10
  220.6 0.6 constant_dynamic-update-slice_fusion.8
  221.9 0.6 constant_dynamic-update-slice_fusion.6
  224.4 0.6 constant_dynamic-update-slice_fusion.2
  225.0 0.6 constant_dynamic-update-slice_fusion.1
  225.7 0.6 constant_dynamic-update-slice_fusion
  226.3 6.3 %all-to-all-done.7 = bf16[32,2,4096]{2,1,0:T(2,128)(2,1)S(1)} async-done(((bf16[32,2,4096]{2,1,0:T(2,128)(2,1)}), bf16[32,2,4096]{2,1,0:T(2,128)(2,1)S(1)}, u32[]{:S(2)}, u32[]{:S(2)}) %all-to-all-start.7) | async-done | bytes 524320 | tf_op jit(solution)/shard_map/all_to_all | solution.py:115
  232.6 8.0 %all-to-all-start.6 = ((bf16[16,2,32,256]{3,1,2,0:T(2,128)(2,1)}), bf16[16,2,32,256]{3,1,2,0:T(2,128)(2,1)S(1)}, u32[]{:S(2)}, u32[]{:S(2)}) async-start(bf16[16,2,32,256]{3,1,2,0:T(2,128)(2,1)} %constant_dynamic-update-slice_fusion), calls=%async_computation.6 | async-start | bytes 1048576 | tf_op jit(solution)/shard_map/all_to_all | solution.py:118
  241.2 1.1 copy.65
  242.2 10.2 %all-to-all-done.6 = bf16[16,2,32,256]{3,1,2,0:T(2,128)(2,1)S(1)} async-done(((bf16[16,2,32,256]{3,1,2,0:T(2,128)(2,1)}), bf16[16,2,32,256]{3,1,2,0:T(2,128)(2,1)S(1)}, u32[]{:S(2)}, u32[]{:S(2)}) %all-to-all-start.6) | async-done | bytes 524320 | tf_op jit(solution)/shard_map/all_to_all | solution.py:118
  252.5 6.9 %all-to-all-start.8 = ((bf16[32,32,256]{2,1,0:T(8,128)(2,1)}), bf16[32,32,256]{2,1,0:T(8,128)(2,1)S(1)}, u32[]{:S(2)}, u32[]{:S(2)}) async-start(bf16[32,32,256]{2,1,0:T(8,128)(2,1)} %copy.65), calls=%async_computation.8 | async-start | bytes 1048576 | tf_op jit(solution)/shard_map/all_to_all | solution.py:125
  259.3 9.4 %multiply_convert_fusion.2 = (bf16[512,1024]{0,1:T(8,128)(2,1)S(1)}, bf16[512,1024]{0,1:T(8,128)(2,1)}) fusion(f32[512]{0:T(512)S(1)} %fusion.70), kind=kLoop, calls=%fused_computation.55 | loop fusion | flops 12058624 | bytes 2099200 | tf_op jit(solution)/shard_map/convert.7
  268.8 0.9 copy.63
  269.7 1.4 all-to-all-done.8
  271.1 2.6 fusion.34
  273.7 2.0 copy.67
  275.8 6.8 %all-to-all-start.9 = ((bf16[2,1024,256]{2,0,1:T(2,128)(2,1)}), bf16[2,1024,256]{2,0,1:T(2,128)(2,1)}, u32[]{:S(2)}, u32[]{:S(2)}) async-start(bf16[2,1024,256]{2,0,1:T(2,128)(2,1)} %copy.67), calls=%async_computation.9 | async-start | bytes 2097152 | tf_op jit(solution)/shard_map/all_to_all | solution.py:138
  282.6 0.8 fusion.75
  283.3 8.8 %collective-permute-start = (bf16[1,64,256]{2,1,0:T(8,128)(2,1)S(1)}, bf16[1,64,256]{2,1,0:T(8,128)(2,1)S(1)}, u32[]{:S(2)}, u32[]{:S(2)}) collective-permute-start(bf16[1,64,256]{2,1,0:T(8,128)(2,1)S(1)} %get-tuple-element.9), channel_id=1, source_target_pairs={{0,16},{16,32},{32,48},{48,64},{64,80},{80,96},{96,112},{112,128},... | collective-permute-start | bytes 98312 | tf_op jit(solution)/shard_map/ppermute | solution.py:15
  292.2 2.2 collective-permute-start.1
  294.4 4.0 %collective-permute-done = bf16[1,64,256]{2,1,0:T(8,128)(2,1)S(1)} collective-permute-done((bf16[1,64,256]{2,1,0:T(8,128)(2,1)S(1)}, bf16[1,64,256]{2,1,0:T(8,128)(2,1)S(1)}, u32[]{:S(2)}, u32[]{:S(2)}) %collective-permute-start) | collective-permute-done | bytes 32800 | tf_op jit(solution)/shard_map/ppermute | solution.py:15
  298.4 8.2 %collective-permute-done.1 = bf16[1,64,256]{2,1,0:T(8,128)(2,1)S(1)} collective-permute-done((bf16[1,64,256]{2,1,0:T(8,128)(2,1)S(1)}, bf16[1,64,256]{2,1,0:T(8,128)(2,1)S(1)}, u32[]{:S(2)}, u32[]{:S(2)}) %collective-permute-start.1) | collective-permute-done | bytes 32800 | tf_op jit(solution)/shard_map/ppermute | solution.py:16
  306.6 1.0 pad_maximum_fusion.5
  307.6 1.9 collective-permute-start.2
  309.6 3.4 %collective-permute-start.3 = (bf16[34,1,256]{2,1,0:T(2,128)(2,1)S(1)}, bf16[34,1,256]{2,1,0:T(2,128)(2,1)S(1)}, u32[]{:S(2)}, u32[]{:S(2)}) collective-permute-start(bf16[34,1,256]{2,1,0:T(2,128)(2,1)S(1)} %get-tuple-element.8), channel_id=1, source_target_pairs={{1,0},{2,1},{3,2},{4,3},{5,4},{6,5},{7,6},{8,7},{9,8},{10,9},{11,1... | collective-permute-start | bytes 52232 | tf_op jit(solution)/shard_map/ppermute | solution.py:16
  313.6 4.6 %collective-permute-done.3 = bf16[34,1,256]{2,1,0:T(2,128)(2,1)S(1)} collective-permute-done((bf16[34,1,256]{2,1,0:T(2,128)(2,1)S(1)}, bf16[34,1,256]{2,1,0:T(2,128)(2,1)S(1)}, u32[]{:S(2)}, u32[]{:S(2)}) %collective-permute-start.3) | collective-permute-done | bytes 17440 | tf_op jit(solution)/shard_map/ppermute | solution.py:16
  318.2 2.3 maximum_maximum_fusion.3
  320.5 2.1 convert_bitcast_fusion
  323.4 5.2 %fusion.14 = bf16[32,64,256]{2,1,0:T(8,128)(2,1)} fusion(bf16[32,64,256]{2,1,0:T(8,128)(2,1)S(1)} %copy-done, f32[16,2,64,256]{3,2,1,0:T(8,128)S(1)} %copy.68, bf16[32,64,256]{2,1,0:T(8,128)(2,1)} %fusion.12, bf16[34,65,256]{2,1,0:T(8,128)(2,1)S(1)} %get-tuple-element.6, bf16[1,64,256]{2,1,0:T(8,128)(2,1)S(1)} %copy-done.9, ...), kind=kLoop, calls=%fused_computation.31 | loop fusion | flops 16777216 | bytes 11609088 | tf_op jit(solution)/shard_map/convert_element_type | solution.py:139
  (81 shorter events, 13.6 us)
Async XLA Ops:
  0.0 3.6 %copy-start = (bf16[32,64,256]{2,1,0:T(8,128)(2,1)S(1)}, bf16[32,64,256]{2,1,0:T(8,128)(2,1)}, u32[]{:S(2)}) copy-start(bf16[32,64,256]{2,1,0:T(8,128)(2,1)} %param.5) | copy-start | bytes 3145732
  0.0 3.6 %copy-start.21 = (f32[256]{0:T(256)S(1)}, f32[256]{0:T(256)}, u32[]{:S(2)}) copy-start(f32[256]{0:T(256)} %param.6) | copy-start | bytes 3076
  5.1 29.4 %all-to-all-start = ((bf16[32,64,256]{2,1,0:T(8,128)(2,1)}), bf16[32,64,256]{2,1,0:T(8,128)(2,1)S(1)}, u32[]{:S(2)}, u32[]{:S(2)}) async-start(bf16[32,64,256]{2,1,0:T(8,128)(2,1)} %fusion.12), calls=%async_computation | async-start | bytes 2097152 | tf_op jit(solution)/shard_map/all_to_all | solution.py:58
  34.5 1.2 copy-start.3
  38.4 19.3 %all-to-all-start.1 = ((bf16[2,512,256]{2,0,1:T(2,128)(2,1)}), bf16[2,512,256]{2,0,1:T(2,128)(2,1)S(1)}, u32[]{:S(2)}, u32[]{:S(2)}) async-start(bf16[2,512,256]{2,0,1:T(2,128)(2,1)} %copy.49), calls=%async_computation.1 | async-start | bytes 1048576 | tf_op jit(solution)/shard_map/all_to_all | solution.py:71
  57.7 17.8 %all-to-all-start.3 = ((bf16[2,512,256]{2,0,1:T(2,128)(2,1)}), bf16[2,512,256]{2,0,1:T(2,128)(2,1)S(1)}, u32[]{:S(2)}, u32[]{:S(2)}) async-start(bf16[2,512,256]{2,0,1:T(2,128)(2,1)} %copy.53), calls=%async_computation.3 | async-start | bytes 1048576 | tf_op jit(solution)/shard_map/all_to_all | solution.py:72
  75.5 34.8 %all-to-all-start.2 = ((bf16[32,32,256]{2,0,1:T(8,128)(2,1)}), bf16[32,32,256]{2,0,1:T(8,128)(2,1)S(1)}, u32[]{:S(2)}, u32[]{:S(2)}) async-start(bf16[32,32,256]{2,0,1:T(8,128)(2,1)} %copy.52), calls=%async_computation.2 | async-start | bytes 1048576 | tf_op jit(solution)/shard_map/all_to_all | solution.py:75
  110.3 0.8 copy-start.5
  111.2 41.6 %all-to-all-start.4 = ((bf16[32,32,256]{2,0,1:T(8,128)(2,1)}), bf16[32,32,256]{2,0,1:T(8,128)(2,1)}, u32[]{:S(2)}, u32[]{:S(2)}) async-start(bf16[32,32,256]{2,0,1:T(8,128)(2,1)} %copy.56), calls=%async_computation.4 | async-start | bytes 1048576 | tf_op jit(solution)/shard_map/all_to_all | solution.py:76
  167.6 0.9 copy-start.4
  168.9 0.9 copy-start.10
  170.9 1.6 copy-start.1
  170.9 2.2 copy-start.2
  178.2 29.3 %all-to-all-start.5 = ((bf16[32,2,4096]{2,1,0:T(2,128)(2,1)}), bf16[32,2,4096]{2,1,0:T(2,128)(2,1)S(1)}, u32[]{:S(2)}, u32[]{:S(2)}) async-start(bf16[32,2,4096]{2,1,0:T(2,128)(2,1)} %reshape.164), calls=%async_computation.5 | async-start | bytes 1048576 | tf_op jit(solution)/shard_map/all_to_all | solution.py:114
  207.5 25.1 %all-to-all-start.7 = ((bf16[32,2,4096]{2,1,0:T(2,128)(2,1)}), bf16[32,2,4096]{2,1,0:T(2,128)(2,1)S(1)}, u32[]{:S(2)}, u32[]{:S(2)}) async-start(bf16[32,2,4096]{2,1,0:T(2,128)(2,1)} %reshape.162), calls=%async_computation.7 | async-start | bytes 1048576 | tf_op jit(solution)/shard_map/all_to_all | solution.py:115
  232.6 19.9 %all-to-all-start.6 = ((bf16[16,2,32,256]{3,1,2,0:T(2,128)(2,1)}), bf16[16,2,32,256]{3,1,2,0:T(2,128)(2,1)S(1)}, u32[]{:S(2)}, u32[]{:S(2)}) async-start(bf16[16,2,32,256]{3,1,2,0:T(2,128)(2,1)} %constant_dynamic-update-slice_fusion), calls=%async_computation.6 | async-start | bytes 1048576 | tf_op jit(solution)/shard_map/all_to_all | solution.py:118
  252.5 18.6 %all-to-all-start.8 = ((bf16[32,32,256]{2,1,0:T(8,128)(2,1)}), bf16[32,32,256]{2,1,0:T(8,128)(2,1)S(1)}, u32[]{:S(2)}, u32[]{:S(2)}) async-start(bf16[32,32,256]{2,1,0:T(8,128)(2,1)} %copy.65), calls=%async_computation.8 | async-start | bytes 1048576 | tf_op jit(solution)/shard_map/all_to_all | solution.py:125
  275.8 37.2 %copy-start.11 = (f32[3,3,256]{2,1,0:T(4,128)S(1)}, f32[3,3,256]{2,1,0:T(4,128)}, u32[]{:S(2)}) copy-start(f32[3,3,256]{2,1,0:T(4,128)} %param.9) | copy-start | bytes 27652
  275.8 44.7 %all-to-all-start.9 = ((bf16[2,1024,256]{2,0,1:T(2,128)(2,1)}), bf16[2,1024,256]{2,0,1:T(2,128)(2,1)}, u32[]{:S(2)}, u32[]{:S(2)}) async-start(bf16[2,1024,256]{2,0,1:T(2,128)(2,1)} %copy.67), calls=%async_computation.9 | async-start | bytes 2097152 | tf_op jit(solution)/shard_map/all_to_all | solution.py:138
  283.3 15.0 %collective-permute-start = (bf16[1,64,256]{2,1,0:T(8,128)(2,1)S(1)}, bf16[1,64,256]{2,1,0:T(8,128)(2,1)S(1)}, u32[]{:S(2)}, u32[]{:S(2)}) collective-permute-start(bf16[1,64,256]{2,1,0:T(8,128)(2,1)S(1)} %get-tuple-element.9), channel_id=1, source_target_pairs={{0,16},{16,32},{32,48},{48,64},{64,80},{80,96},{96,112},{112,128},... | collective-permute-start | bytes 98312 | tf_op jit(solution)/shard_map/ppermute | solution.py:15
  292.2 14.4 %collective-permute-start.1 = (bf16[1,64,256]{2,1,0:T(8,128)(2,1)S(1)}, bf16[1,64,256]{2,1,0:T(8,128)(2,1)S(1)}, u32[]{:S(2)}, u32[]{:S(2)}) collective-permute-start(bf16[1,64,256]{2,1,0:T(8,128)(2,1)S(1)} %get-tuple-element.10), channel_id=1, source_target_pairs={{16,0},{32,16},{48,32},{64,48},{80,64},{96,80},{112,96},{128,112},... | collective-permute-start | bytes 98312 | tf_op jit(solution)/shard_map/ppermute | solution.py:16
  298.4 19.8 %copy-start.6 = (bf16[1,64,256]{2,1,0:T(8,128)(2,1)}, bf16[1,64,256]{2,1,0:T(8,128)(2,1)S(1)}, u32[]{:S(2)}) copy-start(bf16[1,64,256]{2,1,0:T(8,128)(2,1)S(1)} %collective-permute-done) | copy-start | bytes 98308
  306.6 11.6 %copy-start.8 = (bf16[1,64,256]{2,1,0:T(8,128)(2,1)}, bf16[1,64,256]{2,1,0:T(8,128)(2,1)S(1)}, u32[]{:S(2)}) copy-start(bf16[1,64,256]{2,1,0:T(8,128)(2,1)S(1)} %collective-permute-done.1) | copy-start | bytes 98308
  307.6 5.9 %collective-permute-start.2 = (bf16[34,1,256]{2,1,0:T(2,128)(2,1)S(1)}, bf16[34,1,256]{2,1,0:T(2,128)(2,1)S(1)}, u32[]{:S(2)}, u32[]{:S(2)}) collective-permute-start(bf16[34,1,256]{2,1,0:T(2,128)(2,1)S(1)} %get-tuple-element.7), channel_id=1, source_target_pairs={{0,1},{1,2},{2,3},{3,4},{4,5},{5,6},{6,7},{7,8},{8,9},{9,10},{10,1... | collective-permute-start | bytes 52232 | tf_op jit(solution)/shard_map/ppermute | solution.py:15
  309.6 8.6 %collective-permute-start.3 = (bf16[34,1,256]{2,1,0:T(2,128)(2,1)S(1)}, bf16[34,1,256]{2,1,0:T(2,128)(2,1)S(1)}, u32[]{:S(2)}, u32[]{:S(2)}) collective-permute-start(bf16[34,1,256]{2,1,0:T(2,128)(2,1)S(1)} %get-tuple-element.8), channel_id=1, source_target_pairs={{1,0},{2,1},{3,2},{4,3},{5,4},{6,5},{7,6},{8,7},{9,8},{10,9},{11,1... | collective-permute-start | bytes 52232 | tf_op jit(solution)/shard_map/ppermute | solution.py:16
  322.6 0.8 copy-start.7
  322.6 0.8 copy-start.9
  322.6 0.8 copy-start.12
  322.6 0.8 copy-start.13
  322.6 0.7 copy-start.14
  322.6 0.7 copy-start.15
  322.7 0.7 copy-start.16
  322.7 0.7 copy-start.17
  322.7 0.7 copy-start.18
  322.7 0.7 copy-start.19
  322.7 0.7 copy-start.20
